TPU v7x, 32 devices: a whole 2x2x4 slice. The times are simulated.
32 devices in a mesh: branch: 2 (over x), dp: 16 (over z, y, core).
Axes of the slice: x: 2, y: 2, z: 4, core: 2. Of those that a mesh axis runs over, the one named last changes fastest.
Arguments:
- inputs: bfloat16 [96, 816, 512], P('dp'), may hold values from -6 to 6
- window_count: int32 [16], P('dp'), may hold values from 1 to 6, as said below
- branch_blocks: bfloat16 [2, 2, 23552, 512], P('branch', None, 'dp')
- branch_gains: float32 [2, 512], P('branch'), may hold values from 0.1 to 1.9
- branch_biases: float32 [2, 4, 512], P('branch'), may hold values from -2.5 to 2.5
- merge_weight: bfloat16 [1024, 512], replicated, may hold values from -0.1875 to 0.1875
- ff_in: bfloat16 [512, 2048], replicated, may hold values from -0.25 to 0.25
- ff_in_bias: float32 [2048], replicated, may hold values from -2.5 to 2.5
- ff_out: bfloat16 [2048, 512], replicated, may hold values from -0.25 to 0.25
- shared_biases: float32 [4, 512], replicated, may hold values from -2.5 to 2.5
- shared_gains: float32 [2, 512], replicated, may hold values from 0.1 to 1.9
- d_out: bfloat16 [48, 2, 1, 816, 512], P('dp', 'branch'), may hold values from -6 to 6
Outputs:
- layer_out: bfloat16 [48, 2, 1, 816, 512], P('dp', 'branch')
- grad_inputs: bfloat16 [48, 2, 1, 816, 512], P('dp', 'branch')
- grad_branch_blocks: float32 [2, 2, 23552, 512], P('branch', None, 'dp')
- grad_branch_gains: float32 [2, 512], P('branch')
- grad_branch_biases: float32 [2, 4, 512], P('branch')
- grad_merge_weight: float32 [1024, 512], replicated
- grad_ff_in: float32 [512, 2048], replicated
- grad_ff_in_bias: float32 [2048], replicated
- grad_ff_out: float32 [2048, 512], replicated
- grad_shared_biases: float32 [4, 512], replicated
- grad_shared_gains: float32 [2, 512], replicated
Inputs may be any that keep to these rules, and one draw needn't show every extreme that they name: window_count[j] is the number of live windows among windows j * 6 to (j + 1) * 6 - 1, the live ones first; at least one entry equals 6.
All inputs are finite; a program needn't handle non-finite values.
Results may differ from a plain program's by a relative error of at most 0.015.
Values may be sent and summed in bfloat16 or wider, within the bound.
A program may use at most 512 MiB of HBM per device.

v0:
```python
from functools import partial
import jax
import jax.numpy as jnp
from jax import lax
from jax.sharding import PartitionSpec as P

SCALE_A = 12
SCALE_B = 16
MICRO = 3
GRAD_GROUPS = 2
BLOCKS = 92
EPSILON = 1e-05


def layer_norm(values, norm_gain, norm_shift):
    centre = values - jnp.mean(values, axis=-1, keepdims=True)
    spread = jnp.mean(centre * centre, axis=-1, keepdims=True)
    return centre * lax.rsqrt(spread + EPSILON) * norm_gain + norm_shift


def gelu_exact(values):
    return jax.nn.gelu(values, approximate=False)


def column_sum(values):
    return jnp.sum(values.astype(jnp.float32), axis=(0, 1))


def pad_taps(values, tap_total):
    return jnp.pad(values, ((0, 0), (0, tap_total - values.shape[1]), (0, 0)))


def past_windows(values, tap_count, begin, finish):
    batch_size, length, channels = values.shape
    padded = jnp.concatenate(
        [jnp.zeros((batch_size, tap_count - 1, channels), values.dtype), values], axis=1
    )
    offsets = jnp.arange(length)[:, None] + jnp.arange(begin, finish)[None, :]
    return padded[:, offsets, :]


def future_windows(values, tap_count):
    batch_size, length, channels = values.shape
    padded = jnp.concatenate(
        [values, jnp.zeros((batch_size, tap_count - 1, channels), values.dtype)], axis=1
    )
    offsets = jnp.arange(length)[:, None] + (tap_count - 1) - jnp.arange(tap_count)[None, :]
    return padded[:, offsets, :]


def split_blocks(blocks, stride, tap_count):
    return (
        blocks[:stride],
        blocks[stride : stride + tap_count],
        blocks[stride + tap_count : 2 * stride + tap_count],
    )


def branch_forward(stride, tap_total, values, blocks, norm_gain, biases):
    batch_size, length, channels = values.shape
    tap_count = length // stride
    down_weight, iso_weight, up_weight = split_blocks(blocks, stride, tap_count)
    tap_rows = values.reshape(batch_size, tap_count, stride, channels)
    act_full = jnp.tanh(
        jnp.einsum("btrd,rdo->bto", tap_rows, down_weight, preferred_element_type=jnp.float32)
        + biases[0]
    )
    windows = past_windows(act_full.astype(jnp.bfloat16), tap_count, 0, tap_count)
    iso_full = jnp.tanh(
        jnp.einsum("btsd,sdo->bto", windows, iso_weight, preferred_element_type=jnp.float32)
        + biases[1]
    )
    expanded = jnp.einsum(
        "bte,red->btrd",
        iso_full.astype(jnp.bfloat16),
        up_weight,
        preferred_element_type=jnp.float32,
    )
    residual = (
        expanded.reshape(batch_size, length, channels) + biases[2] + values.astype(jnp.float32)
    )
    branch_out = layer_norm(residual, norm_gain, biases[3])
    return (branch_out, residual, pad_taps(act_full, tap_total), pad_taps(iso_full, tap_total))


def branch_backward(
    stride, tap_total, values, grad_branch, residual, act_full, iso_full, blocks, norm_gain, biases
):
    batch_size, length, channels = values.shape
    tap_count = length // stride
    down_weight, iso_weight, up_weight = split_blocks(blocks, stride, tap_count)
    act_used = act_full[:, :tap_count]
    iso_used = iso_full[:, :tap_count]
    unused, norm_back = jax.vjp(layer_norm, residual, norm_gain, biases[3])
    grad_residual, grad_gain, grad_shift = norm_back(grad_branch.astype(jnp.float32))
    grad_expanded = grad_residual.astype(jnp.bfloat16)
    grad_taps = grad_expanded.reshape(batch_size, tap_count, stride, channels)
    grad_iso_out = jnp.einsum(
        "btrd,red->bte", grad_taps, up_weight, preferred_element_type=jnp.float32
    )
    grad_iso = (grad_iso_out * (1.0 - iso_used * iso_used)).astype(jnp.bfloat16)
    grad_act = jnp.einsum(
        "btso,sdo->btd",
        future_windows(grad_iso, tap_count),
        iso_weight,
        preferred_element_type=jnp.float32,
    )
    grad_down = (grad_act * (1.0 - act_used * act_used)).astype(jnp.bfloat16)
    grad_rows = jnp.einsum(
        "bto,rdo->btrd", grad_down, down_weight, preferred_element_type=jnp.float32
    )
    grad_values = grad_residual + grad_rows.reshape(batch_size, length, channels)
    vectors = jnp.stack(
        [
            grad_gain,
            column_sum(grad_down),
            column_sum(grad_iso),
            column_sum(grad_expanded),
            grad_shift,
        ]
    )
    return (
        grad_values,
        vectors,
        pad_taps(grad_down, tap_total),
        pad_taps(grad_iso, tap_total),
        grad_expanded,
    )


def group_grads(
    group_index, stride, values, activation, isometric, grad_down, grad_iso, grad_expanded
):
    batch_size, length, channels = values.shape
    tap_count = length // stride
    per_group = BLOCKS // GRAD_GROUPS
    first_block = group_index * per_group
    end_block = first_block + per_group
    pieces = []
    covered = 0
    begin, finish = (max(first_block, 0), min(end_block, stride))
    if begin < finish:
        tap_rows = values.reshape(batch_size, tap_count, stride, channels)
        pieces.append(
            jnp.einsum(
                "btrd,bto->rdo",
                tap_rows,
                grad_down[:, :tap_count],
                preferred_element_type=jnp.float32,
            )
        )
        covered += finish - begin
    begin, finish = (max(first_block, stride), min(end_block, stride + tap_count))
    windows = past_windows(activation[:, :tap_count], tap_count, begin - stride, finish - stride)
    pieces.append(
        jnp.einsum(
            "btsd,bto->sdo", windows, grad_iso[:, :tap_count], preferred_element_type=jnp.float32
        )
    )
    covered += finish - begin
    begin, finish = (max(first_block, stride + tap_count), min(end_block, 2 * stride + tap_count))
    if begin < finish:
        grad_taps = grad_expanded.reshape(batch_size, tap_count, stride, channels)
        pieces.append(
            jnp.einsum(
                "bte,btrd->red",
                isometric[:, :tap_count],
                grad_taps,
                preferred_element_type=jnp.float32,
            )
        )
        covered += finish - begin
    if covered < per_group:
        pieces.append(jnp.zeros((per_group - covered, channels, channels), jnp.float32))
    return jnp.concatenate(pieces, axis=0).reshape(per_group * channels, channels)


def group_term(
    group_index, branch_index, values, activation, isometric, grad_down, grad_iso, grad_expanded
):
    return lax.cond(
        branch_index == 0,
        partial(group_grads, group_index, SCALE_A),
        partial(group_grads, group_index, SCALE_B),
        values,
        activation,
        isometric,
        grad_down,
        grad_iso,
        grad_expanded,
    )


def per_device(
    inputs,
    window_count,
    branch_blocks,
    branch_gains,
    branch_biases,
    merge_weight,
    ff_in,
    ff_in_bias,
    ff_out,
    shared_biases,
    shared_gains,
    d_out,
):
    branch_index = lax.axis_index("branch")
    slot_total, length, channels = inputs.shape
    per_micro = slot_total // MICRO
    half_micro = per_micro // 2
    tap_total = max(length // SCALE_A, length // SCALE_B)
    gathered = lax.all_gather(branch_blocks, "dp", axis=2, tiled=True)
    blocks = gathered.reshape(-1, channels, channels)
    norm_gain = branch_gains[0]
    biases = branch_biases[0]
    live_count = window_count[0]
    forward_pair = (
        partial(branch_forward, SCALE_A, tap_total),
        partial(branch_forward, SCALE_B, tap_total),
    )
    backward_pair = (
        partial(branch_backward, SCALE_A, tap_total),
        partial(branch_backward, SCALE_B, tap_total),
    )
    shared_totals = [
        jnp.zeros(merge_weight.shape, jnp.float32),
        jnp.zeros(ff_in.shape, jnp.float32),
        jnp.zeros(ff_in_bias.shape, jnp.float32),
        jnp.zeros(ff_out.shape, jnp.float32),
        jnp.zeros(shared_biases.shape, jnp.float32),
        jnp.zeros(shared_gains.shape, jnp.float32),
    ]
    vector_total = jnp.zeros((5, channels), jnp.float32)
    kept_parts = []
    outputs = []
    input_parts = []
    for micro_index in range(MICRO):
        start = micro_index * per_micro
        values = inputs[start : start + per_micro]
        branch_out, residual, act_full, iso_full = lax.cond(
            branch_index == 0, forward_pair[0], forward_pair[1], values, blocks, norm_gain, biases
        )
        joined = lax.all_to_all(
            branch_out.astype(jnp.bfloat16), "branch", split_axis=0, concat_axis=2, tiled=True
        )
        merged = (
            jnp.einsum("btk,ko->bto", joined, merge_weight, preferred_element_type=jnp.float32)
            + shared_biases[0]
        )
        normed_full, norm_one_back = jax.vjp(layer_norm, merged, shared_gains[0], shared_biases[1])
        normed = normed_full.astype(jnp.bfloat16)
        inner_pre = (
            jnp.einsum("btd,df->btf", normed, ff_in, preferred_element_type=jnp.float32)
            + ff_in_bias
        )
        hidden_full, gelu_back = jax.vjp(gelu_exact, inner_pre)
        hidden = hidden_full.astype(jnp.bfloat16)
        outer_pre = (
            jnp.einsum("btf,fd->btd", hidden, ff_out, preferred_element_type=jnp.float32)
            + shared_biases[2]
        )
        result, norm_two_back = jax.vjp(
            layer_norm, merged + outer_pre, shared_gains[1], shared_biases[3]
        )
        window_ids = start + branch_index * half_micro + jnp.arange(half_micro)
        alive_mask = (window_ids < live_count).astype(jnp.float32)[:, None, None]
        outputs.append((result * alive_mask).astype(jnp.bfloat16))
        cotangent = d_out[micro_index, 0].astype(jnp.float32) * alive_mask
        grad_sum, grad_gain_two, grad_shift_two = norm_two_back(cotangent)
        grad_outer = grad_sum.astype(jnp.bfloat16)
        grad_hidden = jnp.einsum(
            "btd,fd->btf", grad_outer, ff_out, preferred_element_type=jnp.float32
        )
        grad_inner = gelu_back(grad_hidden)[0].astype(jnp.bfloat16)
        grad_normed = jnp.einsum(
            "btf,df->btd", grad_inner, ff_in, preferred_element_type=jnp.float32
        )
        grad_norm_in, grad_gain_one, grad_shift_one = norm_one_back(grad_normed)
        grad_merged = (grad_sum + grad_norm_in).astype(jnp.bfloat16)
        grad_joined = jnp.einsum(
            "bto,ko->btk", grad_merged, merge_weight, preferred_element_type=jnp.float32
        ).astype(jnp.bfloat16)
        terms = (
            jnp.einsum("btk,bto->ko", joined, grad_merged, preferred_element_type=jnp.float32),
            jnp.einsum("btd,btf->df", normed, grad_inner, preferred_element_type=jnp.float32),
            column_sum(grad_inner),
            jnp.einsum("btf,btd->fd", hidden, grad_outer, preferred_element_type=jnp.float32),
            jnp.stack(
                [column_sum(grad_merged), grad_shift_one, column_sum(grad_outer), grad_shift_two]
            ),
            jnp.stack([grad_gain_one, grad_gain_two]),
        )
        shared_totals = [running + addend for running, addend in zip(shared_totals, terms)]
        grad_branch = lax.all_to_all(grad_joined, "branch", split_axis=2, concat_axis=0, tiled=True)
        grad_values, vectors, grad_down, grad_iso, grad_expanded = lax.cond(
            branch_index == 0,
            backward_pair[0],
            backward_pair[1],
            values,
            grad_branch,
            residual,
            act_full,
            iso_full,
            blocks,
            norm_gain,
            biases,
        )
        vector_total = vector_total + vectors
        summed_values = lax.psum_scatter(
            grad_values.astype(jnp.bfloat16), "branch", scatter_dimension=0, tiled=True
        )
        input_parts.append(summed_values)
        activation = act_full.astype(jnp.bfloat16)
        isometric = iso_full.astype(jnp.bfloat16)
        kept_parts.append((activation, isometric, grad_down, grad_iso, grad_expanded))
    activation_all = jnp.concatenate([entry[0] for entry in kept_parts], axis=0)
    isometric_all = jnp.concatenate([entry[1] for entry in kept_parts], axis=0)
    grad_down_all = jnp.concatenate([entry[2] for entry in kept_parts], axis=0)
    grad_iso_all = jnp.concatenate([entry[3] for entry in kept_parts], axis=0)
    grad_expanded_all = jnp.concatenate([entry[4] for entry in kept_parts], axis=0)
    block_result = []
    for group_index in range(GRAD_GROUPS):
        term = group_term(
            group_index,
            branch_index,
            inputs,
            activation_all,
            isometric_all,
            grad_down_all,
            grad_iso_all,
            grad_expanded_all,
        )
        block_result.append(lax.psum_scatter(term, "dp", scatter_dimension=0, tiled=True))
    vector_full = jnp.where((jnp.arange(2) == branch_index)[:, None, None], vector_total[None], 0.0)
    summed = lax.psum(
        (
            shared_totals[0],
            shared_totals[1],
            shared_totals[2],
            shared_totals[3],
            shared_totals[4],
            shared_totals[5],
            vector_full,
        ),
        ("branch", "dp"),
    )
    own_vectors = lax.dynamic_slice_in_dim(summed[6], branch_index, 1, 0)
    layer_out = jnp.stack(outputs)[:, None]
    grad_inputs = jnp.stack(input_parts)[:, None]
    grad_blocks = jnp.stack(block_result)[None]
    return (
        layer_out,
        grad_inputs,
        grad_blocks,
        own_vectors[:, 0],
        own_vectors[:, 1:],
        summed[0],
        summed[1],
        summed[2],
        summed[3],
        summed[4],
        summed[5],
    )


def solution(mesh):
    placed = (
        P("dp", None, None),
        P("dp"),
        P("branch", None, "dp", None),
        P("branch", None),
        P("branch", None, None),
        P(),
        P(),
        P(),
        P(),
        P(),
        P(),
        P("dp", "branch", None, None, None),
    )
    return jax.shard_map(
        per_device,
        mesh=mesh,
        in_specs=placed,
        out_specs=(
            P("dp", "branch", None, None, None),
            P("dp", "branch", None, None, None),
            P("branch", None, "dp", None),
            P("branch", None),
            P("branch", None, None),
            P(),
            P(),
            P(),
            P(),
            P(),
            P(),
        ),
        check_vma=False,
    )
```

profile of v0, /device:TPU:0, one launch (start us, length us, event | category | flops | bytes accessed | tf_op | source)
XLA Modules:
  0.0 2379.5 jit_solution(8030178385065969234)
XLA Ops:
  7.9 4.8 fusion.653
  15.6 233.9 %all-gather.2.cloned.1.call-done = bf16[1,2,23552,512]{3,2,1,0:T(8,128)(2,1)} async-done(((bf16[1,2,1472,512]{3,2,1,0:T(8,128)(2,1)}), bf16[1,2,23552,512]{3,2,1,0:T(8,128)(2,1)}) %all-gather.2.cloned.1.call-update) | async-done | bytes 48234512 | tf_op jit(solution)/shard_map/all_gather | solution.py:213
  249.5 94.2 %conditional.10 = (bf16[2,816,512]{2,1,0:T(8,128)(2,1)}, f32[2,816,512]{2,1,0:T(8,128)}, f32[2,68,512]{2,1,0:T(8,128)S(1)}, f32[2,68,512]{2,1,0:T(8,128)}) conditional(s32[]{:T(128)} %convert_element_type.450, (bf16[2,816,512]{2,0,1:T(2,128)(2,1)}, bf16[92,512,512]{2,1,0:T(8,128)(2,1)}, f32[4,512]{1,0:T(4,128)S(1)}, ...), branch_computations={%region_20.0_spmd, %region_23.0_spmd} | conditional | flops 6570222080 | bytes 131432216 | solution.py:241
  262.0 27.4 %gather_fusion.9 = bf16[4624,2,512]{2,1,0:T(2,128)(2,1)} fusion(bf16[2,135,512]{2,0,1:T(2,128)(2,1)S(1)} %concatenate.55.clone, s32[5120]{0:T(1024)S(1)} %pad_clamp_fusion.5), kind=kCustom, calls=%fused_computation.5 | custom fusion | bytes 18958400 | tf_op jit(solution)/shard_map/cond/branch_1_fun/gather | solution.py:39
  289.4 33.7 %fusion.251 = f32[2,68,512]{2,1,0:T(8,128)S(1)} fusion(bf16[92,512,512]{2,1,0:T(8,128)(2,1)} %get-tuple-element.277, bf16[2,68,68,512]{3,0,2,1:T(2,128)(2,1)} %bitcast.970, f32[512]{0:T(512)S(1)} %bitcast.1114), kind=kOutput, calls=%fused_computation.171 | convolution fusion | flops 4848685056 | bytes 45402112 | tf_op jit(solution)/shard_map/cond/branch_1_fun/btsd,sdo->bto/dot_general | solution.py:70
  352.8 87.1 %conditional.9 = (bf16[2,816,512]{2,1,0:T(8,128)(2,1)}, f32[2,816,512]{2,1,0:T(8,128)}, f32[2,68,512]{2,1,0:T(8,128)S(1)}, f32[2,68,512]{2,1,0:T(8,128)}) conditional(s32[]{:T(128)} %convert_element_type.450, (bf16[2,816,512]{2,0,1:T(2,128)(2,1)}, bf16[92,512,512]{2,1,0:T(8,128)(2,1)}, f32[4,512]{1,0:T(4,128)S(1)}, ...), branch_computations={%region_10.0_spmd, %region_13.0_spmd} | conditional | flops 6570222080 | bytes 131432216 | solution.py:241
  358.1 27.4 %gather_fusion.7 = bf16[4624,2,512]{2,1,0:T(2,128)(2,1)} fusion(bf16[2,135,512]{2,0,1:T(2,128)(2,1)S(1)} %concatenate.53.clone, s32[5120]{0:T(1024)S(1)} %pad_clamp_fusion.3), kind=kCustom, calls=%fused_computation.3 | custom fusion | bytes 18958400 | tf_op jit(solution)/shard_map/cond/branch_1_fun/gather | solution.py:39
  385.5 33.7 %fusion.165 = f32[2,68,512]{2,1,0:T(8,128)S(1)} fusion(bf16[92,512,512]{2,1,0:T(8,128)(2,1)} %get-tuple-element.269, bf16[2,68,68,512]{3,0,2,1:T(2,128)(2,1)} %bitcast.971, f32[512]{0:T(512)S(1)} %bitcast.1115), kind=kOutput, calls=%fused_computation.117 | convolution fusion | flops 4848685056 | bytes 45402112 | tf_op jit(solution)/shard_map/cond/branch_1_fun/btsd,sdo->bto/dot_general | solution.py:70
  439.9 4.8 all-to-all-start.1
  450.9 87.1 %conditional.8 = (bf16[2,816,512]{2,1,0:T(8,128)(2,1)}, f32[2,816,512]{2,1,0:T(8,128)}, f32[2,68,512]{2,1,0:T(8,128)S(1)}, f32[2,68,512]{2,1,0:T(8,128)}) conditional(s32[]{:T(128)} %convert_element_type.450, (bf16[2,816,512]{2,0,1:T(2,128)(2,1)}, bf16[92,512,512]{2,1,0:T(8,128)(2,1)}, f32[4,512]{1,0:T(4,128)S(1)}, ...), branch_computations={%region_0.3_spmd, %region_3.6_spmd} | conditional | flops 6570222080 | bytes 131432216 | solution.py:241
  456.3 27.4 %gather_fusion.5 = bf16[4624,2,512]{2,1,0:T(2,128)(2,1)} fusion(bf16[2,135,512]{2,0,1:T(2,128)(2,1)S(1)} %concatenate.51.clone, s32[5120]{0:T(1024)S(1)} %pad_clamp_fusion.1), kind=kCustom, calls=%fused_computation.1 | custom fusion | bytes 18958400 | tf_op jit(solution)/shard_map/cond/branch_1_fun/gather | solution.py:39
  483.7 33.7 %fusion.79 = f32[2,68,512]{2,1,0:T(8,128)S(1)} fusion(bf16[92,512,512]{2,1,0:T(8,128)(2,1)} %get-tuple-element.261, bf16[2,68,68,512]{3,0,2,1:T(2,128)(2,1)} %bitcast.972, f32[512]{0:T(512)S(1)} %bitcast.1116), kind=kOutput, calls=%fused_computation.63 | convolution fusion | flops 4848685056 | bytes 45402112 | tf_op jit(solution)/shard_map/cond/branch_1_fun/btsd,sdo->bto/dot_general | solution.py:70
  555.7 14.1 all-to-all-done
  580.5 61.1 %multiply_convert_fusion.2 = (bf16[816,2048]{1,0:T(8,128)(2,1)S(1)}, f32[816,2048]{1,0:T(8,128)}, bf16[816,2048]{1,0:T(8,128)(2,1)S(1)}, f32[816,2048]{1,0:T(8,1...) fusion(f32[2048]{0:T(1024)S(1)} %copy-done.153, f32[816,2048]{1,0:T(8,128)S(1)} %fusion.625, ...), kind=kOutput, calls=%fused_computation.503 | convolution fusion | flops 2044256256 | bytes 53922176 | tf_op jit(solution)/shard_map/btd,df->btf/dot_general | solution.py:254
  658.4 8.5 convert_reduce_fusion.25
  669.7 8.1 convert_reduce_fusion.24
  680.6 8.3 convert_reduce_fusion.26
  699.3 6.4 copy.332
  706.3 11.8 reduce.90
  722.5 23.8 %all_to_all.99 = bf16[2,2,208896]{2,1,0:T(2,128)(2,1)S(1)} all-to-all(bf16[2,2,208896]{2,1,0:T(2,128)(2,1)} %reshape.2176), channel_id=1, replica_groups=mesh['branch'=2,'dp'=16] {'branch'}, dimensions={0} | all-to-all | bytes 3342336 | tf_op jit(solution)/shard_map/all_to_all | solution.py:295
  753.8 4.9 copy.394
  758.8 78.8 %conditional.13 = (f32[5,512]{1,0:T(8,128)S(1)}, bf16[2,68,512]{2,1,0:T(8,128)(2,1)S(1)}, bf16[2,68,512]{2,1,0:T(8,128)(2,1)S(1)}, bf16[2,816,512]{2,1,0:T(8,128...) conditional(s32[]{:T(128)} %convert_element_type.450, (f32[2,816,512]{2,1,0:T(8,128)}, ...), branch_computations={%region_84.94_spmd, %region_94.104_spmd} | conditional | flops 6586659328 | bytes 125944344 | solution.py:296
  775.6 5.0 convert_reduce_fusion.22
  780.9 27.4 %gather_fusion.15 = bf16[4624,2,512]{2,1,0:T(2,128)(2,1)} fusion(bf16[2,135,512]{2,0,1:T(2,128)(2,1)S(1)} %concatenate.61.clone, s32[5120]{0:T(1024)S(1)} %pad_clamp_fusion.11), kind=kCustom, calls=%fused_computation.11 | custom fusion | bytes 18958400 | tf_op jit(solution)/shard_map/cond/branch_1_fun/gather | solution.py:48
  808.3 19.1 convert_reduce_fusion.23
  827.5 5.0 fusion.502
  837.7 4.8 add_convert_fusion.3
  848.2 6.4 copy.324
  854.7 11.8 reduce.92
  870.8 22.9 all_to_all.100
  901.2 4.9 copy.392
  906.2 86.7 %conditional.11 = (f32[5,512]{1,0:T(8,128)S(1)}, bf16[2,68,512]{2,1,0:T(8,128)(2,1)S(1)}, bf16[2,68,512]{2,1,0:T(8,128)(2,1)S(1)}, bf16[2,816,512]{2,1,0:T(8,128...) conditional(s32[]{:T(128)} %convert_element_type.450, (f32[2,816,512]{2,1,0:T(8,128)}, ...), branch_computations={%region_34.44_spmd, %region_44.54_spmd} | conditional | flops 6586659328 | bytes 125944344 | solution.py:296
  930.7 5.0 convert_reduce_fusion.6
  936.0 27.4 %gather_fusion.11 = bf16[4624,2,512]{2,1,0:T(2,128)(2,1)} fusion(bf16[2,135,512]{2,0,1:T(2,128)(2,1)S(1)} %concatenate.57.clone, s32[5120]{0:T(1024)S(1)} %pad_clamp_fusion.7), kind=kCustom, calls=%fused_computation.7 | custom fusion | bytes 18958400 | tf_op jit(solution)/shard_map/cond/branch_1_fun/gather | solution.py:48
  963.4 19.1 convert_reduce_fusion.7
  982.5 5.0 fusion.310
  993.0 4.8 add_convert_fusion.5
  1003.5 6.4 copy.328
  1010.0 11.8 reduce.91
  1026.1 22.0 all_to_all.101
  1055.6 4.9 copy.393
  1060.6 87.0 %conditional.12 = (f32[5,512]{1,0:T(8,128)S(1)}, bf16[2,68,512]{2,1,0:T(8,128)(2,1)}, bf16[2,68,512]{2,1,0:T(8,128)(2,1)S(1)}, bf16[2,816,512]{2,1,0:T(8,128)(2,...) conditional(s32[]{:T(128)} %convert_element_type.450, (f32[2,816,512]{2,1,0:T(8,128)}, ...), branch_computations={%region_59.69_spmd, %region_69.79_spmd} | conditional | flops 6586659328 | bytes 124838360 | solution.py:296
  1084.8 5.0 convert_reduce_fusion.14
  1090.1 27.4 %gather_fusion.13 = bf16[4624,2,512]{2,1,0:T(2,128)(2,1)} fusion(bf16[2,135,512]{2,0,1:T(2,128)(2,1)S(1)} %concatenate.59.clone, s32[5120]{0:T(1024)S(1)} %pad_clamp_fusion.9), kind=kCustom, calls=%fused_computation.9 | custom fusion | bytes 18958400 | tf_op jit(solution)/shard_map/cond/branch_1_fun/gather | solution.py:48
  1117.5 19.9 convert_reduce_fusion.15
  1137.5 5.0 fusion.406
  1156.7 5.3 pad_maximum_fusion.3
  1162.0 87.3 %conditional.15 = (f32[46,512,512]{2,1,0:T(8,128)}) conditional(s32[]{:T(128)} %convert_element_type.450, (bf16[6,68,512]{2,0,1:T(8,128)(2,1)S(1)}, bf16[6,68,512]{2,1,0:T(8,128)(2,1)S(1)}, bf16[6,816,512]{2,1,0:T(8,128)(2,1)}, bf16[6,68,512]{2,1,0:T(8,128)(2,1)S(1)}) %tuple.367, (bf16[6,68,512]{2,0,1:T(8,128)(2,1)S(1)}, ...), branch_computations={%region_108.109_spmd, %region_109.110_spmd} | conditional | flops 9851908096 | bytes 204500416 | solution.py:181
  1162.5 9.0 reshape.1925
  1171.5 13.2 fusion.578
  1184.7 10.6 gather_fusion.3
  1195.3 20.5 fusion.573
  1215.8 33.5 %pad_maximum_fusion.2 = f32[46,512,512]{2,1,0:T(8,128)} fusion(f32[12,512,512]{2,1,0:T(8,128)} %fusion.578, f32[34,512,512]{2,1,0:T(8,128)} %fusion.573), kind=kLoop, calls=%fused_computation.453 | loop fusion | flops 12058624 | bytes 96468992 | tf_op jit(solution)/shard_map/cond/branch_1_fun/concatenate | solution.py:175
  1251.2 112.8 %conditional.14 = (f32[46,512,512]{2,1,0:T(8,128)}) conditional(s32[]{:T(128)} %convert_element_type.450, (bf16[6,816,512]{2,1,0:T(8,128)(2,1)}, bf16[6,68,512]{2,1,0:T(8,128)(2,1)S(1)}, bf16[6,68,512]{2,0,1:T(8,128)(2,1)S(1)}, bf16[6,68,512]{2,1,0:T(8,128)(2,1)S(1)}) %tuple.369, (bf16[6,816,512]{2,1,0:T(8,128)(2,1)}, ...), branch_computations={%region_105.106_spmd, %region_106.107_spmd} | conditional | flops 9851908096 | bytes 204500128 | solution.py:181
  1260.0 9.6 reshape.1923
  1269.6 28.5 %fusion.560 = f32[12,512,512]{2,1,0:T(8,128)} fusion(bf16[6,68,12,512]{3,2,1,0:T(8,128)(2,1)} %reshape.1923, bf16[6,68,512]{2,1,0:T(8,128)(2,1)S(1)} %get-tuple-element.321), kind=kOutput, calls=%fused_computation.436 | convolution fusion | flops 2566914048 | bytes 18014208 | tf_op jit(solution)/shard_map/cond/branch_1_fun/btrd,bto->rdo/dot_general | solution.py:145
  1298.1 11.4 gather_fusion.1
  1309.6 20.8 fusion.555
  1330.4 33.3 %pad_maximum_fusion.1 = f32[46,512,512]{2,1,0:T(8,128)} fusion(f32[34,512,512]{2,1,0:T(8,128)} %fusion.555, f32[12,512,512]{2,1,0:T(8,128)} %fusion.560), kind=kLoop, calls=%fused_computation.430 | loop fusion | flops 12058624 | bytes 96468992 | tf_op jit(solution)/shard_map/cond/branch_1_fun/concatenate | solution.py:175
  1397.2 45.0 %all-reduce.28 = (f32[2,5,512]{2,1,0:T(8,128)S(1)}, f32[2048]{0:T(1024)}, f32[4,512]{1,0:T(4,128)}, f32[2,512]{1,0:T(2,128)}) all-reduce(f32[2,5,512]{2,1,0:T(8,128)S(1)} %broadcast_select_fusion, f32[2048]{0:T(1024)S(1)} %add_add_fusion.19, f32[4,512]{1,0:T(4,128)S(1)} %fusion.613, ...), channel_id=1, replica_groups=mesh['branch'=2,'dp'=16] {'branch','dp'}, use_global_device_ids=true, to_apply=%region_111.112 | all-reduce | flops 10240 | bytes 81920 | tf_op jit(solution)/shard_map/psum | solution.py:336
  1446.8 253.1 %reduce-scatter.14.cloned.1.call-done = f32[1472,512]{1,0:T(8,128)} async-done(((f32[23552,512]{1,0:T(8,128)}), f32[1472,512]{1,0:T(8,128)}) %reduce-scatter.14.cloned.1.call-update) | async-done | bytes 3014672 | tf_op jit(solution)/shard_map/reduce_scatter | solution.py:334
  1699.9 453.7 %reduce-scatter.12.cloned.1.call-done = f32[1472,512]{1,0:T(8,128)} async-done(((f32[23552,512]{1,0:T(8,128)}), f32[1472,512]{1,0:T(8,128)}) %reduce-scatter.12.cloned.1.call-update) | async-done | bytes 3014672 | tf_op jit(solution)/shard_map/reduce_scatter | solution.py:334
  2153.6 6.1 maximum_bitcast_fusion
  2159.7 203.9 %all-reduce.32.cloned.1.call-done = (f32[1024,512]{1,0:T(8,128)}, f32[512,2048]{1,0:T(8,128)}, f32[2048,512]{1,0:T(8,128)}) async-done(((f32[1024,512]{1,0:T(8,128)}, f32[512,2048]{1,0:T(8,128)}, f32[2048,512]{1,0:T(8,128)}), (f32[1024,512]{1,0:T(8,128)}, f32[512,2048]{1,0:T(8,128)}, f32[2048,512]{1,0:T(8,128)})) %all-reduce.32.cloned.1.call-update) | async-done | bytes 10485776 | tf_op jit(solution)/shard_map/psum | solution.py:336
  (554 shorter events, 323.9 us)
Async XLA Ops:
  7.2 568.0 %copy-start = (bf16[512,2048]{1,0:T(8,128)(2,1)S(1)}, bf16[512,2048]{1,0:T(8,128)(2,1)}, u32[]{:S(2)}) copy-start(bf16[512,2048]{1,0:T(8,128)(2,1)} %param.34) | copy-start | bytes 6291460
  7.2 242.3 %all-gather.2.cloned.1.call-start = ((), (), s32[]{:S(2)}) async-start(), calls=%async_computation.11 | async-start | bytes 51249152 | tf_op jit(solution)/shard_map/all_gather | solution.py:213
  12.7 236.8 %copy-start.71 = (f32[1,512]{1,0:T(1,128)S(1)}, f32[1,512]{1,0:T(1,128)}, u32[]{:S(2)}) copy-start(f32[1,512]{1,0:T(1,128)} %param.31) | copy-start | bytes 6148
  12.7 236.8 %copy-start.87 = (f32[1,4,512]{2,1,0:T(4,128)S(1)}, f32[1,4,512]{2,1,0:T(4,128)}, u32[]{:S(2)}) copy-start(f32[1,4,512]{2,1,0:T(4,128)} %param.32) | copy-start | bytes 24580
  343.8 9.0 copy-start.73
  343.8 96.1 %all-to-all-start.2 = ((bf16[2,816,512]{2,1,0:T(8,128)(2,1)}), bf16[2,816,512]{2,1,0:T(8,128)(2,1)}, u32[]{:S(2)}, u32[]{:S(2)}) async-start(bf16[2,816,512]{2,1,0:T(8,128)(2,1)} %get-tuple-element.375), calls=%async_computation.2 | async-start | bytes 3342336 | tf_op jit(solution)/shard_map/all_to_all | solution.py:244
  439.9 10.5 copy-start.76
  439.9 10.4 copy-start.133
  439.9 104.1 %all-to-all-start.1 = ((bf16[2,816,512]{2,1,0:T(8,128)(2,1)}), bf16[2,816,512]{2,1,0:T(8,128)(2,1)}, u32[]{:S(2)}, u32[]{:S(2)}) async-start(bf16[2,816,512]{2,1,0:T(8,128)(2,1)} %get-tuple-element.374), calls=%async_computation.1 | async-start | bytes 3342336 | tf_op jit(solution)/shard_map/all_to_all | solution.py:244
  445.3 247.5 %copy-start.88 = (f32[1,512]{1,0:T(1,128)}, f32[1,512]{1,0:T(1,128)S(1)}, u32[]{:S(2)}) copy-start(f32[1,512]{1,0:T(1,128)S(1)} %get-tuple-element.817) | copy-start | bytes 6148
  450.9 128.7 %copy-start.95 = (f32[1,512]{1,0:T(1,128)}, f32[1,512]{1,0:T(1,128)S(1)}, u32[]{:S(2)}) copy-start(f32[1,512]{1,0:T(1,128)S(1)} %get-tuple-element.813) | copy-start | bytes 6148
  544.1 33.5 %copy-start.110 = (f32[816]{0:T(1024)}, f32[816]{0:T(1024)S(1)}, u32[]{:S(2)}) copy-start(f32[816]{0:T(1024)S(1)} %broadcast_multiply_fusion.13) | copy-start | bytes 9796
  544.1 25.7 %all-to-all-start = ((bf16[2,816,512]{2,1,0:T(8,128)(2,1)}), bf16[2,816,512]{2,1,0:T(8,128)(2,1)}, u32[]{:S(2)}, u32[]{:S(2)}) async-start(bf16[2,816,512]{2,1,0:T(8,128)(2,1)} %get-tuple-element.373), calls=%async_computation | async-start | bytes 3342336 | tf_op jit(solution)/shard_map/all_to_all | solution.py:244
  548.8 894.6 %reduce-scatter.10.cloned.1.call-start = ((), (), s32[]{:S(2)}) async-start(), calls=%async_computation.14 | async-start | bytes 2506752 | tf_op jit(solution)/shard_map/reduce_scatter | solution.py:310
  554.1 21.1 copy-start.90
  555.3 18.2 copy-start.113
  555.7 17.9 copy-start.115
  555.7 21.9 copy-start.123
  555.7 19.5 copy-start.97
  574.7 118.1 %copy-start.13 = (f32[816,512]{1,0:T(8,128)}, f32[816,512]{1,0:T(8,128)S(1)}, u32[]{:S(2)}) copy-start(f32[816,512]{1,0:T(8,128)S(1)} %get-tuple-element.829) | copy-start | bytes 5013508
  574.7 118.1 %copy-start.93 = (f32[816]{0:T(1024)}, f32[816]{0:T(1024)S(1)}, u32[]{:S(2)}) copy-start(f32[816]{0:T(1024)S(1)} %broadcast_multiply_fusion.17) | copy-start | bytes 9796
  575.1 117.7 %copy-start.100 = (f32[816]{0:T(1024)}, f32[816]{0:T(1024)S(1)}, u32[]{:S(2)}) copy-start(f32[816]{0:T(1024)S(1)} %fusion.615) | copy-start | bytes 9796
  580.5 61.1 %copy-start.154 = (f32[816,2048]{1,0:T(8,128)}, f32[816,2048]{1,0:T(8,128)S(1)}, u32[]{:S(2)}) copy-start(f32[816,2048]{1,0:T(8,128)S(1)} %fusion.625) | copy-start | bytes 20054020
  580.5 61.2 %copy-start.147 = (f32[1,512]{1,0:T(1,128)S(1)}, f32[1,512]{1,0:T(1,128)}, u32[]{:S(2)}) copy-start(f32[1,512]{1,0:T(1,128)} %get-tuple-element.815) | copy-start | bytes 6148
  580.5 61.2 %copy-start.148 = (bf16[2048,512]{1,0:T(8,128)(2,1)S(1)}, bf16[2048,512]{1,0:T(8,128)(2,1)}, u32[]{:S(2)}) copy-start(bf16[2048,512]{1,0:T(8,128)(2,1)} %param.36) | copy-start | bytes 6291460
  641.7 5.2 copy-start.158
  656.4 23.4 copy-start.21
  656.4 10.5 copy-start.119
  658.4 8.5 copy-start.80
  669.7 8.1 copy-start.33
  680.6 8.3 copy-start.82
  680.6 8.3 copy-start.91
  680.6 8.3 copy-start.98
  680.6 8.3 copy-start.111
  680.6 8.3 copy-start.124
  750.2 8.6 copy-start.45
  750.2 8.6 copy-start.72
  750.2 8.6 copy-start.74
  780.6 27.7 %copy-start.55 = (bf16[2,68,512]{2,1,0:T(8,128)(2,1)}, bf16[2,68,512]{2,1,0:T(8,128)(2,1)S(1)}, u32[]{:S(2)}) copy-start(bf16[2,68,512]{2,1,0:T(8,128)(2,1)S(1)} %get-tuple-element.882) | copy-start | bytes 417796 | tf_op jit(solution)/shard_map/cond
  827.4 5.0 copy-start.63
  837.7 4.9 copy-start.57
  837.7 4.9 copy-start.65
  837.7 4.8 copy-start.102
  837.7 4.9 copy-start.22
  842.6 600.8 %reduce-scatter.6.cloned.1.call-start = ((), (), s32[]{:S(2)}) async-start(), calls=%async_computation.12 | async-start | bytes 2506752 | tf_op jit(solution)/shard_map/reduce_scatter | solution.py:310
  897.6 8.6 copy-start.50
  897.6 8.6 copy-start.79
  935.6 27.7 %copy-start.59 = (bf16[2,68,512]{2,1,0:T(8,128)(2,1)}, bf16[2,68,512]{2,1,0:T(8,128)(2,1)S(1)}, u32[]{:S(2)}) copy-start(bf16[2,68,512]{2,1,0:T(8,128)(2,1)S(1)} %get-tuple-element.906) | copy-start | bytes 417796 | tf_op jit(solution)/shard_map/cond
  982.5 5.0 copy-start.67
  992.9 4.9 copy-start.69
  993.0 4.9 copy-start.104
  993.0 5.0 copy-start.126
  993.0 5.0 copy-start.20
  993.0 5.0 copy-start.120
  997.9 445.5 %reduce-scatter.8.cloned.1.call-start = ((), (), s32[]{:S(2)}) async-start(), calls=%async_computation.13 | async-start | bytes 2506752 | tf_op jit(solution)/shard_map/reduce_scatter | solution.py:310
  1052.0 8.6 copy-start.48
  1052.0 8.6 copy-start.77
  1089.8 27.7 %copy-start.61 = (bf16[2,68,512]{2,1,0:T(8,128)(2,1)}, bf16[2,68,512]{2,1,0:T(8,128)(2,1)S(1)}, u32[]{:S(2)}) copy-start(bf16[2,68,512]{2,1,0:T(8,128)(2,1)S(1)} %get-tuple-element.894) | copy-start | bytes 417796 | tf_op jit(solution)/shard_map/cond
  1147.7 5.1 copy-start.46
  1152.4 547.5 %reduce-scatter.14.cloned.1.call-start = ((), (), s32[]{:S(2)}) async-start(), calls=%async_computation.16 | async-start | bytes 51249152 | tf_op jit(solution)/shard_map/reduce_scatter | solution.py:334
  1156.7 5.3 copy-start.109
  1249.3 904.3 %reduce-scatter.12.cloned.1.call-start = ((), (), s32[]{:S(2)}) async-start(), calls=%async_computation.15 | async-start | bytes 51249152 | tf_op jit(solution)/shard_map/reduce_scatter | solution.py:334
  1364.1 999.4 %all-reduce.32.cloned.1.call-start = ((), (), s32[]{:S(2)}) async-start(), calls=%async_computation.17 | async-start | bytes 20971520 | tf_op jit(solution)/shard_map/psum | solution.py:336
  2366.8 5.7 copy-start.1
  (102 other events, 281.6 us)
Sparse Core Ops, SparseCore 0:
  9.6 239.8 all-gather.1
  842.7 26.2 reduce-scatter.9
  998.0 26.2 reduce-scatter.5
  1152.5 26.2 reduce-scatter.7
  1249.4 450.4 reduce-scatter.13
  1704.7 448.9 reduce-scatter.11
  2160.9 202.6 all-reduce.31
where the time goes:
time: 2390 us; the launch traced here: 2380 us
  waiting for transfers between devices  1160 us (49%)
  matrix products  437 us (18%)
  local copies, waits for them, and re-layouts  374 us (16%)
  other arithmetic  227 us (9%)
  blocking collectives  114 us (5%)
  loops' own time  35.9 us (2%)
    reduce_scatter x2, waiting for transfers between devices, per_device(): lax.psum_scatter(term, 'dp', scatter_dimension=0, tiled=True)  707 us
    all_gather x1, waiting for transfers between devices, per_device(): gathered = lax.all_gather(branch_blocks, 'dp', axis=2, tiled=True)  234 us
    psum x1, waiting for transfers between devices, per_device(): lax.psum((shared_totals[0], shared_totals[1], shared_totals[2], shared_to...  204 us
    gather x5, local copies, waits for them, and re-layouts, past_windows(): return padded[:, offsets, :]  104 us
    dot_general x3, matrix products, branch_forward(): jnp.einsum('btsd,sdo->bto', windows, iso_weight, preferred_element_type=j...  101 us
    gather x3, local copies, waits for them, and re-layouts, future_windows(): return padded[:, offsets, :]  82.2 us
    unnamed x301, local copies, waits for them, and re-layouts  69.1 us
    all_to_all x3, blocking collectives, per_device(): lax.all_to_all(grad_joined, 'branch', split_axis=2, concat_axis=0, tiled=...  68.8 us
  transfers between devices with their start and end apart: 10, of which 5 were waited for; matrix products, arithmetic and copies ran while one was open for 29% of the time, Pallas kernels for 0%

commit v1 on v0

--- a/solution.py
+++ b/solution.py
@@ -292,7 +292,12 @@
             jnp.stack([grad_gain_one, grad_gain_two]),
         )
         shared_totals = [running + addend for running, addend in zip(shared_totals, terms)]
-        grad_branch = lax.all_to_all(grad_joined, "branch", split_axis=2, concat_axis=0, tiled=True)
+        grad_branch = jnp.concatenate(
+            lax.all_to_all(
+                jnp.stack(jnp.split(grad_joined, lax.axis_size("branch"), axis=2)), "branch", 0, 0
+            ),
+            axis=0,
+        )
         grad_values, vectors, grad_down, grad_iso, grad_expanded = lax.cond(
             branch_index == 0,
             backward_pair[0],

time: 2390 us -> 2310 us (0.967)
  local copies, waits for them, and re-layouts: 374 us -> 301 us
  other arithmetic: 227 us -> 194 us
  blocking collectives: 114 us -> 143 us
    unnamed x301 -> x291, local copies, waits for them, and re-layouts: 69.1 us -> 29.5 us
    unnamed x4 -> x1, other arithmetic: 37 us -> 1.73 us
    all_to_all x3, blocking collectives: 68.8 us -> 98.9 us  [per_device(): lax.all_to_all(jnp.stack(jnp.split(grad_joined, lax.axis_size('branch'),...]
  transfers between devices with their start and end apart: 10 -> 10, of which waited for: 5 -> 5; matrix products, arithmetic and copies ran while one was open for 29% -> 27% of each run, Pallas kernels for 0% -> 0%
where the time goes in v1:
time: 2310 us; the launch traced here: 2300 us
  waiting for transfers between devices  1160 us (50%)
  matrix products  437 us (19%)
  local copies, waits for them, and re-layouts  301 us (13%)
  other arithmetic  194 us (8%)
  blocking collectives  143 us (6%)
  loops' own time  35.8 us (2%)
    reduce_scatter x2, waiting for transfers between devices, per_device(): lax.psum_scatter(term, 'dp', scatter_dimension=0, tiled=True)  710 us
    all_gather x1, waiting for transfers between devices, per_device(): gathered = lax.all_gather(branch_blocks, 'dp', axis=2, tiled=True)  234 us
    psum x1, waiting for transfers between devices, per_device(): lax.psum((shared_totals[0], shared_totals[1], shared_totals[2], shared_to...  204 us
    gather x5, local copies, waits for them, and re-layouts, past_windows(): return padded[:, offsets, :]  104 us
    dot_general x3, matrix products, branch_forward(): jnp.einsum('btsd,sdo->bto', windows, iso_weight, preferred_element_type=j...  101 us
    all_to_all x3, blocking collectives, per_device(): lax.all_to_all(jnp.stack(jnp.split(grad_joined, lax.axis_size('branch'),...  98.9 us
    gather x3, local copies, waits for them, and re-layouts, future_windows(): return padded[:, offsets, :]  82.2 us
    concatenate x2, other arithmetic, group_grads(): jnp.concatenate(pieces, axis=0).reshape(per_group * channels, channels)  67 us
  transfers between devices with their start and end apart: 10, of which 5 were waited for; matrix products, arithmetic and copies ran while one was open for 27% of the time, Pallas kernels for 0%

profile of v1, /device:TPU:0, one launch (start us, length us, event | category | flops | bytes accessed | tf_op | source)
XLA Modules:
  0.0 2304.9 jit_solution(14280436743063928825)
XLA Ops:
  7.9 4.8 fusion.653
  15.6 233.9 %all-gather.2.cloned.1.call-done = bf16[1,2,23552,512]{3,2,1,0:T(8,128)(2,1)} async-done(((bf16[1,2,1472,512]{3,2,1,0:T(8,128)(2,1)}), bf16[1,2,23552,512]{3,2,1,0:T(8,128)(2,1)}) %all-gather.2.cloned.1.call-update) | async-done | bytes 48234512 | tf_op jit(solution)/shard_map/all_gather | solution.py:213
  249.5 94.2 %conditional.10 = (bf16[2,816,512]{2,1,0:T(8,128)(2,1)}, f32[2,816,512]{2,1,0:T(8,128)}, f32[2,68,512]{2,1,0:T(8,128)S(1)}, f32[2,68,512]{2,1,0:T(8,128)}) conditional(s32[]{:T(128)} %convert_element_type.450, (bf16[2,816,512]{2,0,1:T(2,128)(2,1)}, bf16[92,512,512]{2,1,0:T(8,128)(2,1)}, f32[4,512]{1,0:T(4,128)S(1)}, ...), branch_computations={%region_20.0_spmd, %region_23.0_spmd} | conditional | flops 6570222080 | bytes 131432216 | solution.py:241
  257.2 4.5 fusion.652
  262.0 27.4 %gather_fusion.9 = bf16[4624,2,512]{2,1,0:T(2,128)(2,1)} fusion(bf16[2,135,512]{2,0,1:T(2,128)(2,1)S(1)} %concatenate.55.clone, s32[5120]{0:T(1024)S(1)} %pad_clamp_fusion.5), kind=kCustom, calls=%fused_computation.5 | custom fusion | bytes 18958400 | tf_op jit(solution)/shard_map/cond/branch_1_fun/gather | solution.py:39
  289.4 33.7 %fusion.251 = f32[2,68,512]{2,1,0:T(8,128)S(1)} fusion(bf16[92,512,512]{2,1,0:T(8,128)(2,1)} %get-tuple-element.277, bf16[2,68,68,512]{3,0,2,1:T(2,128)(2,1)} %bitcast.961, f32[512]{0:T(512)S(1)} %bitcast.1102), kind=kOutput, calls=%fused_computation.171 | convolution fusion | flops 4848685056 | bytes 45402112 | tf_op jit(solution)/shard_map/cond/branch_1_fun/btsd,sdo->bto/dot_general | solution.py:70
  343.8 4.7 all-to-all-start.2
  352.8 87.1 %conditional.9 = (bf16[2,816,512]{2,1,0:T(8,128)(2,1)}, f32[2,816,512]{2,1,0:T(8,128)}, f32[2,68,512]{2,1,0:T(8,128)S(1)}, f32[2,68,512]{2,1,0:T(8,128)}) conditional(s32[]{:T(128)} %convert_element_type.450, (bf16[2,816,512]{2,0,1:T(2,128)(2,1)}, bf16[92,512,512]{2,1,0:T(8,128)(2,1)}, f32[4,512]{1,0:T(4,128)S(1)}, ...), branch_computations={%region_10.0_spmd, %region_13.0_spmd} | conditional | flops 6570222080 | bytes 131432216 | solution.py:241
  353.3 4.5 fusion.648
  358.1 27.4 %gather_fusion.7 = bf16[4624,2,512]{2,1,0:T(2,128)(2,1)} fusion(bf16[2,135,512]{2,0,1:T(2,128)(2,1)S(1)} %concatenate.53.clone, s32[5120]{0:T(1024)S(1)} %pad_clamp_fusion.3), kind=kCustom, calls=%fused_computation.3 | custom fusion | bytes 18958400 | tf_op jit(solution)/shard_map/cond/branch_1_fun/gather | solution.py:39
  385.5 33.7 %fusion.165 = f32[2,68,512]{2,1,0:T(8,128)S(1)} fusion(bf16[92,512,512]{2,1,0:T(8,128)(2,1)} %get-tuple-element.269, bf16[2,68,68,512]{3,0,2,1:T(2,128)(2,1)} %bitcast.962, f32[512]{0:T(512)S(1)} %bitcast.1103), kind=kOutput, calls=%fused_computation.117 | convolution fusion | flops 4848685056 | bytes 45402112 | tf_op jit(solution)/shard_map/cond/branch_1_fun/btsd,sdo->bto/dot_general | solution.py:70
  439.9 4.8 all-to-all-start.1
  450.9 87.1 %conditional.8 = (bf16[2,816,512]{2,1,0:T(8,128)(2,1)}, f32[2,816,512]{2,1,0:T(8,128)}, f32[2,68,512]{2,1,0:T(8,128)S(1)}, f32[2,68,512]{2,1,0:T(8,128)}) conditional(s32[]{:T(128)} %convert_element_type.450, (bf16[2,816,512]{2,0,1:T(2,128)(2,1)}, bf16[92,512,512]{2,1,0:T(8,128)(2,1)}, f32[4,512]{1,0:T(4,128)S(1)}, ...), branch_computations={%region_0.3_spmd, %region_3.6_spmd} | conditional | flops 6570222080 | bytes 131432216 | solution.py:241
  451.5 4.5 fusion.644
  456.3 27.4 %gather_fusion.5 = bf16[4624,2,512]{2,1,0:T(2,128)(2,1)} fusion(bf16[2,135,512]{2,0,1:T(2,128)(2,1)S(1)} %concatenate.51.clone, s32[5120]{0:T(1024)S(1)} %pad_clamp_fusion.1), kind=kCustom, calls=%fused_computation.1 | custom fusion | bytes 18958400 | tf_op jit(solution)/shard_map/cond/branch_1_fun/gather | solution.py:39
  483.7 33.7 %fusion.79 = f32[2,68,512]{2,1,0:T(8,128)S(1)} fusion(bf16[92,512,512]{2,1,0:T(8,128)(2,1)} %get-tuple-element.261, bf16[2,68,68,512]{3,0,2,1:T(2,128)(2,1)} %bitcast.963, f32[512]{0:T(512)S(1)} %bitcast.1104), kind=kOutput, calls=%fused_computation.63 | convolution fusion | flops 4848685056 | bytes 45402112 | tf_op jit(solution)/shard_map/cond/branch_1_fun/btsd,sdo->bto/dot_general | solution.py:70
  544.1 4.6 all-to-all-start
  555.7 14.1 all-to-all-done
  580.5 61.1 %multiply_convert_fusion.2 = (bf16[816,2048]{1,0:T(8,128)(2,1)S(1)}, f32[816,2048]{1,0:T(8,128)}, bf16[816,2048]{1,0:T(8,128)(2,1)S(1)}, f32[816,2048]{1,0:T(8,1...) fusion(f32[2048]{0:T(1024)S(1)} %copy-done.153, f32[816,2048]{1,0:T(8,128)S(1)} %fusion.625, ...), kind=kOutput, calls=%fused_computation.503 | convolution fusion | flops 2044256256 | bytes 53922176 | tf_op jit(solution)/shard_map/btd,df->btf/dot_general | solution.py:254
  657.4 8.5 convert_reduce_fusion.25
  668.8 8.1 convert_reduce_fusion.24
  679.7 8.3 convert_reduce_fusion.26
  698.4 22.6 all_to_all.60
  721.1 79.3 %conditional.12 = (f32[5,512]{1,0:T(8,128)S(1)}, bf16[2,68,512]{2,1,0:T(8,128)(2,1)S(1)}, bf16[2,68,512]{2,1,0:T(8,128)(2,1)S(1)}, bf16[2,816,512]{2,1,0:T(8,128...) conditional(s32[]{:T(128)} %convert_element_type.450, (f32[2,816,512]{2,1,0:T(8,128)}, ...), branch_computations={%region_59.69_spmd, %region_69.79_spmd} | conditional | flops 6586659328 | bytes 125944344 | solution.py:301
  738.1 5.0 convert_reduce_fusion.14
  743.4 27.4 %gather_fusion.13 = bf16[4624,2,512]{2,1,0:T(2,128)(2,1)} fusion(bf16[2,135,512]{2,0,1:T(2,128)(2,1)S(1)} %concatenate.59.clone, s32[5120]{0:T(1024)S(1)} %pad_clamp_fusion.9), kind=kCustom, calls=%fused_computation.9 | custom fusion | bytes 18958400 | tf_op jit(solution)/shard_map/cond/branch_1_fun/gather | solution.py:48
  770.8 19.3 convert_reduce_fusion.15
  790.2 5.0 fusion.406
  800.4 4.8 add_convert_fusion.4
  810.6 37.7 %all_to_all.61 = bf16[2,1,816,512]{3,2,1,0:T(8,128)(2,1)S(1)} all-to-all(bf16[2,1,816,512]{3,2,1,0:T(8,128)(2,1)S(1)} %pad_maximum_fusion.4), channel_id=1, replica_groups=mesh['branch'=2,'dp'=16] {'branch'}, dimensions={0} | all-to-all | bytes 3342336 | tf_op jit(solution)/shard_map/all_to_all | solution.py:296
  848.3 87.2 %conditional.11 = (f32[5,512]{1,0:T(8,128)S(1)}, bf16[2,68,512]{2,1,0:T(8,128)(2,1)S(1)}, bf16[2,68,512]{2,1,0:T(8,128)(2,1)S(1)}, bf16[2,816,512]{2,1,0:T(8,128...) conditional(s32[]{:T(128)} %convert_element_type.450, (f32[2,816,512]{2,1,0:T(8,128)}, ...), branch_computations={%region_34.44_spmd, %region_44.54_spmd} | conditional | flops 6586659328 | bytes 125944344 | solution.py:301
  873.2 5.0 convert_reduce_fusion.6
  878.5 27.4 %gather_fusion.11 = bf16[4624,2,512]{2,1,0:T(2,128)(2,1)} fusion(bf16[2,135,512]{2,0,1:T(2,128)(2,1)S(1)} %concatenate.57.clone, s32[5120]{0:T(1024)S(1)} %pad_clamp_fusion.7), kind=kCustom, calls=%fused_computation.7 | custom fusion | bytes 18958400 | tf_op jit(solution)/shard_map/cond/branch_1_fun/gather | solution.py:48
  905.9 19.4 convert_reduce_fusion.7
  925.3 5.0 fusion.310
  935.5 4.8 add_convert_fusion.5
  945.8 38.5 %all_to_all.62 = bf16[2,1,816,512]{3,2,1,0:T(8,128)(2,1)S(1)} all-to-all(bf16[2,1,816,512]{3,2,1,0:T(8,128)(2,1)S(1)} %pad_maximum_fusion.6), channel_id=1, replica_groups=mesh['branch'=2,'dp'=16] {'branch'}, dimensions={0} | all-to-all | bytes 3342336 | tf_op jit(solution)/shard_map/all_to_all | solution.py:296
  984.4 87.8 %conditional.13 = (f32[5,512]{1,0:T(8,128)S(1)}, bf16[2,68,512]{2,1,0:T(8,128)(2,1)}, bf16[2,68,512]{2,1,0:T(8,128)(2,1)S(1)}, bf16[2,816,512]{2,1,0:T(8,128)(2,...) conditional(s32[]{:T(128)} %convert_element_type.450, (f32[2,816,512]{2,1,0:T(8,128)}, ...), branch_computations={%region_84.94_spmd, %region_94.104_spmd} | conditional | flops 6586659328 | bytes 124838360 | solution.py:301
  1001.6 4.3 convert_reduce_fusion.21
  1009.3 5.0 convert_reduce_fusion.22
  1014.6 27.4 %gather_fusion.15 = bf16[4624,2,512]{2,1,0:T(2,128)(2,1)} fusion(bf16[2,135,512]{2,0,1:T(2,128)(2,1)S(1)} %concatenate.61.clone, s32[5120]{0:T(1024)S(1)} %pad_clamp_fusion.11), kind=kCustom, calls=%fused_computation.11 | custom fusion | bytes 18958400 | tf_op jit(solution)/shard_map/cond/branch_1_fun/gather | solution.py:48
  1042.0 20.0 convert_reduce_fusion.23
  1062.0 5.1 fusion.502
  1072.2 4.7 add_convert_fusion.3
  1081.2 5.0 pad_maximum_fusion.3
  1086.2 87.3 %conditional.15 = (f32[46,512,512]{2,1,0:T(8,128)}) conditional(s32[]{:T(128)} %convert_element_type.450, (bf16[6,68,512]{2,0,1:T(8,128)(2,1)S(1)}, bf16[6,68,512]{2,1,0:T(8,128)(2,1)S(1)}, bf16[6,816,512]{2,1,0:T(8,128)(2,1)}, bf16[6,68,512]{2,1,0:T(8,128)(2,1)S(1)}) %tuple.344, (bf16[6,68,512]{2,0,1:T(8,128)(2,1)S(1)}, ...), branch_computations={%region_108.109_spmd, %region_109.110_spmd} | conditional | flops 9851908096 | bytes 204500416 | solution.py:181
  1086.7 9.0 reshape.1931
  1095.8 13.2 fusion.578
  1109.0 10.6 gather_fusion.3
  1119.5 20.5 fusion.573
  1140.0 33.5 %pad_maximum_fusion.2 = f32[46,512,512]{2,1,0:T(8,128)} fusion(f32[12,512,512]{2,1,0:T(8,128)} %fusion.578, f32[34,512,512]{2,1,0:T(8,128)} %fusion.573), kind=kLoop, calls=%fused_computation.453 | loop fusion | flops 12058624 | bytes 96468992 | tf_op jit(solution)/shard_map/cond/branch_1_fun/concatenate | solution.py:175
  1175.5 113.0 %conditional.14 = (f32[46,512,512]{2,1,0:T(8,128)}) conditional(s32[]{:T(128)} %convert_element_type.450, (bf16[6,816,512]{2,1,0:T(8,128)(2,1)}, bf16[6,68,512]{2,1,0:T(8,128)(2,1)S(1)}, bf16[6,68,512]{2,0,1:T(8,128)(2,1)S(1)}, bf16[6,68,512]{2,1,0:T(8,128)(2,1)S(1)}) %tuple.346, (bf16[6,816,512]{2,1,0:T(8,128)(2,1)}, ...), branch_computations={%region_105.106_spmd, %region_106.107_spmd} | conditional | flops 9851908096 | bytes 204500128 | solution.py:181
  1184.3 9.6 reshape.1929
  1193.8 28.2 %fusion.560 = f32[12,512,512]{2,1,0:T(8,128)} fusion(bf16[6,68,12,512]{3,2,1,0:T(8,128)(2,1)} %reshape.1929, bf16[6,68,512]{2,1,0:T(8,128)(2,1)S(1)} %get-tuple-element.321), kind=kOutput, calls=%fused_computation.436 | convolution fusion | flops 2566914048 | bytes 18014208 | tf_op jit(solution)/shard_map/cond/branch_1_fun/btrd,bto->rdo/dot_general | solution.py:145
  1222.0 11.6 gather_fusion.1
  1233.7 20.8 fusion.555
  1254.5 33.5 %pad_maximum_fusion.1 = f32[46,512,512]{2,1,0:T(8,128)} fusion(f32[34,512,512]{2,1,0:T(8,128)} %fusion.555, f32[12,512,512]{2,1,0:T(8,128)} %fusion.560), kind=kLoop, calls=%fused_computation.430 | loop fusion | flops 12058624 | bytes 96468992 | tf_op jit(solution)/shard_map/cond/branch_1_fun/concatenate | solution.py:175
  1306.6 4.6 add_add_fusion.6
  1311.2 4.6 add_add_fusion.7
  1320.6 43.9 %all-reduce.28 = (f32[2,5,512]{2,1,0:T(8,128)S(1)}, f32[2048]{0:T(1024)}, f32[4,512]{1,0:T(4,128)}, f32[2,512]{1,0:T(2,128)}) all-reduce(f32[2,5,512]{2,1,0:T(8,128)S(1)} %broadcast_select_fusion, f32[2048]{0:T(1024)S(1)} %add_add_fusion.19, f32[4,512]{1,0:T(4,128)S(1)} %fusion.613, ...), channel_id=1, replica_groups=mesh['branch'=2,'dp'=16] {'branch','dp'}, use_global_device_ids=true, to_apply=%region_111.112 | all-reduce | flops 10240 | bytes 81920 | tf_op jit(solution)/shard_map/psum | solution.py:341
  1369.2 255.5 %reduce-scatter.14.cloned.1.call-done = f32[1472,512]{1,0:T(8,128)} async-done(((f32[23552,512]{1,0:T(8,128)}), f32[1472,512]{1,0:T(8,128)}) %reduce-scatter.14.cloned.1.call-update) | async-done | bytes 3014672 | tf_op jit(solution)/shard_map/reduce_scatter | solution.py:339
  1624.7 454.2 %reduce-scatter.12.cloned.1.call-done = f32[1472,512]{1,0:T(8,128)} async-done(((f32[23552,512]{1,0:T(8,128)}), f32[1472,512]{1,0:T(8,128)}) %reduce-scatter.12.cloned.1.call-update) | async-done | bytes 3014672 | tf_op jit(solution)/shard_map/reduce_scatter | solution.py:339
  2078.9 6.1 maximum_bitcast_fusion
  2085.0 203.9 %all-reduce.32.cloned.1.call-done = (f32[1024,512]{1,0:T(8,128)}, f32[512,2048]{1,0:T(8,128)}, f32[2048,512]{1,0:T(8,128)}) async-done(((f32[1024,512]{1,0:T(8,128)}, f32[512,2048]{1,0:T(8,128)}, f32[2048,512]{1,0:T(8,128)}), (f32[1024,512]{1,0:T(8,128)}, f32[512,2048]{1,0:T(8,128)}, f32[2048,512]{1,0:T(8,128)})) %all-reduce.32.cloned.1.call-update) | async-done | bytes 10485776 | tf_op jit(solution)/shard_map/psum | solution.py:341
  (541 shorter events, 245.3 us)
Async XLA Ops:
  7.2 568.0 %copy-start = (bf16[512,2048]{1,0:T(8,128)(2,1)S(1)}, bf16[512,2048]{1,0:T(8,128)(2,1)}, u32[]{:S(2)}) copy-start(bf16[512,2048]{1,0:T(8,128)(2,1)} %param.34) | copy-start | bytes 6291460
  7.2 242.3 %all-gather.2.cloned.1.call-start = ((), (), s32[]{:S(2)}) async-start(), calls=%async_computation.11 | async-start | bytes 51249152 | tf_op jit(solution)/shard_map/all_gather | solution.py:213
  12.7 236.8 %copy-start.71 = (f32[1,512]{1,0:T(1,128)S(1)}, f32[1,512]{1,0:T(1,128)}, u32[]{:S(2)}) copy-start(f32[1,512]{1,0:T(1,128)} %param.31) | copy-start | bytes 6148
  12.7 236.8 %copy-start.87 = (f32[1,4,512]{2,1,0:T(4,128)S(1)}, f32[1,4,512]{2,1,0:T(4,128)}, u32[]{:S(2)}) copy-start(f32[1,4,512]{2,1,0:T(4,128)} %param.32) | copy-start | bytes 24580
  343.8 9.0 copy-start.73
  343.8 96.1 %all-to-all-start.2 = ((bf16[2,816,512]{2,1,0:T(8,128)(2,1)}), bf16[2,816,512]{2,1,0:T(8,128)(2,1)}, u32[]{:S(2)}, u32[]{:S(2)}) async-start(bf16[2,816,512]{2,1,0:T(8,128)(2,1)} %get-tuple-element.375), calls=%async_computation.2 | async-start | bytes 3342336 | tf_op jit(solution)/shard_map/all_to_all | solution.py:244
  439.9 10.5 copy-start.75
  439.9 10.4 copy-start.133
  439.9 104.1 %all-to-all-start.1 = ((bf16[2,816,512]{2,1,0:T(8,128)(2,1)}), bf16[2,816,512]{2,1,0:T(8,128)(2,1)}, u32[]{:S(2)}, u32[]{:S(2)}) async-start(bf16[2,816,512]{2,1,0:T(8,128)(2,1)} %get-tuple-element.374), calls=%async_computation.1 | async-start | bytes 3342336 | tf_op jit(solution)/shard_map/all_to_all | solution.py:244
  445.3 246.6 %copy-start.88 = (f32[1,512]{1,0:T(1,128)}, f32[1,512]{1,0:T(1,128)S(1)}, u32[]{:S(2)}) copy-start(f32[1,512]{1,0:T(1,128)S(1)} %get-tuple-element.681) | copy-start | bytes 6148
  450.9 128.7 %copy-start.95 = (f32[1,512]{1,0:T(1,128)}, f32[1,512]{1,0:T(1,128)S(1)}, u32[]{:S(2)}) copy-start(f32[1,512]{1,0:T(1,128)S(1)} %get-tuple-element.677) | copy-start | bytes 6148
  544.1 33.5 %copy-start.110 = (f32[816]{0:T(1024)}, f32[816]{0:T(1024)S(1)}, u32[]{:S(2)}) copy-start(f32[816]{0:T(1024)S(1)} %broadcast_multiply_fusion.13) | copy-start | bytes 9796
  544.1 25.7 %all-to-all-start = ((bf16[2,816,512]{2,1,0:T(8,128)(2,1)}), bf16[2,816,512]{2,1,0:T(8,128)(2,1)}, u32[]{:S(2)}, u32[]{:S(2)}) async-start(bf16[2,816,512]{2,1,0:T(8,128)(2,1)} %get-tuple-element.373), calls=%async_computation | async-start | bytes 3342336 | tf_op jit(solution)/shard_map/all_to_all | solution.py:244
  548.7 816.9 %reduce-scatter.8.cloned.1.call-start = ((), (), s32[]{:S(2)}) async-start(), calls=%async_computation.13 | async-start | bytes 2506752 | tf_op jit(solution)/shard_map/reduce_scatter | solution.py:315
  554.0 21.1 copy-start.90
  555.3 18.2 copy-start.113
  555.6 17.9 copy-start.115
  555.7 21.9 copy-start.123
  555.7 19.4 copy-start.97
  574.7 117.2 %copy-start.13 = (f32[816,512]{1,0:T(8,128)}, f32[816,512]{1,0:T(8,128)S(1)}, u32[]{:S(2)}) copy-start(f32[816,512]{1,0:T(8,128)S(1)} %get-tuple-element.693) | copy-start | bytes 5013508
  574.7 117.2 %copy-start.93 = (f32[816]{0:T(1024)}, f32[816]{0:T(1024)S(1)}, u32[]{:S(2)}) copy-start(f32[816]{0:T(1024)S(1)} %broadcast_multiply_fusion.17) | copy-start | bytes 9796
  575.1 116.8 %copy-start.100 = (f32[816]{0:T(1024)}, f32[816]{0:T(1024)S(1)}, u32[]{:S(2)}) copy-start(f32[816]{0:T(1024)S(1)} %fusion.615) | copy-start | bytes 9796
  580.5 61.2 %copy-start.154 = (f32[816,2048]{1,0:T(8,128)}, f32[816,2048]{1,0:T(8,128)S(1)}, u32[]{:S(2)}) copy-start(f32[816,2048]{1,0:T(8,128)S(1)} %fusion.625) | copy-start | bytes 20054020
  580.5 61.2 %copy-start.147 = (f32[1,512]{1,0:T(1,128)S(1)}, f32[1,512]{1,0:T(1,128)}, u32[]{:S(2)}) copy-start(f32[1,512]{1,0:T(1,128)} %get-tuple-element.679) | copy-start | bytes 6148
  580.5 61.2 %copy-start.148 = (bf16[2048,512]{1,0:T(8,128)(2,1)S(1)}, bf16[2048,512]{1,0:T(8,128)(2,1)}, u32[]{:S(2)}) copy-start(bf16[2048,512]{1,0:T(8,128)(2,1)} %param.36) | copy-start | bytes 6291460
  641.7 5.2 copy-start.158
  653.5 14.4 copy-start.21
  653.5 14.4 copy-start.119
  656.4 22.4 copy-start.19
  657.4 8.6 copy-start.79
  668.8 8.2 copy-start.33
  679.7 8.4 copy-start.81
  679.7 8.4 copy-start.91
  679.7 8.4 copy-start.98
  679.7 8.4 copy-start.111
  679.7 8.4 copy-start.124
  698.2 22.8 copy-start.47
  698.3 22.8 copy-start.72
  698.3 22.8 copy-start.76
  743.1 27.7 %copy-start.55 = (bf16[2,68,512]{2,1,0:T(8,128)(2,1)}, bf16[2,68,512]{2,1,0:T(8,128)(2,1)S(1)}, u32[]{:S(2)}) copy-start(bf16[2,68,512]{2,1,0:T(8,128)(2,1)S(1)} %get-tuple-element.758) | copy-start | bytes 417796 | tf_op jit(solution)/shard_map/cond
  790.1 5.0 copy-start.63
  800.4 4.9 copy-start.57
  800.4 4.9 copy-start.65
  800.4 4.9 copy-start.20
  805.2 560.4 %reduce-scatter.6.cloned.1.call-start = ((), (), s32[]{:S(2)}) async-start(), calls=%async_computation.12 | async-start | bytes 2506752 | tf_op jit(solution)/shard_map/reduce_scatter | solution.py:315
  810.4 37.9 %copy-start.50 = (f32[2,68,512]{2,1,0:T(8,128)S(1)}, f32[2,68,512]{2,1,0:T(8,128)}, u32[]{:S(2)}) copy-start(f32[2,68,512]{2,1,0:T(8,128)} %get-tuple-element.377) | copy-start | bytes 835588
  810.4 37.9 %copy-start.78 = (f32[2,68,512]{2,1,0:T(8,128)S(1)}, f32[2,68,512]{2,1,0:T(8,128)}, u32[]{:S(2)}) copy-start(f32[2,68,512]{2,1,0:T(8,128)} %copy-done.77) | copy-start | bytes 835588
  878.2 27.7 %copy-start.59 = (bf16[2,68,512]{2,1,0:T(8,128)(2,1)}, bf16[2,68,512]{2,1,0:T(8,128)(2,1)S(1)}, u32[]{:S(2)}) copy-start(bf16[2,68,512]{2,1,0:T(8,128)(2,1)S(1)} %get-tuple-element.770) | copy-start | bytes 417796 | tf_op jit(solution)/shard_map/cond
  925.3 5.0 copy-start.67
  935.5 4.9 copy-start.69
  935.5 4.9 copy-start.104
  935.5 5.0 copy-start.126
  935.5 5.0 copy-start.22
  935.5 5.0 copy-start.120
  940.4 425.3 %reduce-scatter.10.cloned.1.call-start = ((), (), s32[]{:S(2)}) async-start(), calls=%async_computation.14 | async-start | bytes 2506752 | tf_op jit(solution)/shard_map/reduce_scatter | solution.py:315
  945.6 38.7 %copy-start.45 = (f32[2,68,512]{2,1,0:T(8,128)S(1)}, f32[2,68,512]{2,1,0:T(8,128)}, u32[]{:S(2)}) copy-start(f32[2,68,512]{2,1,0:T(8,128)} %get-tuple-element.387) | copy-start | bytes 835588
  945.6 38.7 %copy-start.74 = (f32[2,68,512]{2,1,0:T(8,128)S(1)}, f32[2,68,512]{2,1,0:T(8,128)}, u32[]{:S(2)}) copy-start(f32[2,68,512]{2,1,0:T(8,128)} %copy-done.73) | copy-start | bytes 835588
  1014.3 27.7 %copy-start.61 = (bf16[2,68,512]{2,1,0:T(8,128)(2,1)}, bf16[2,68,512]{2,1,0:T(8,128)(2,1)S(1)}, u32[]{:S(2)}) copy-start(bf16[2,68,512]{2,1,0:T(8,128)(2,1)S(1)} %get-tuple-element.746) | copy-start | bytes 417796 | tf_op jit(solution)/shard_map/cond
  1072.2 6.4 copy-start.48
  1077.0 547.7 %reduce-scatter.14.cloned.1.call-start = ((), (), s32[]{:S(2)}) async-start(), calls=%async_computation.16 | async-start | bytes 51249152 | tf_op jit(solution)/shard_map/reduce_scatter | solution.py:339
  1081.2 5.0 copy-start.109
  1173.6 905.4 %reduce-scatter.12.cloned.1.call-start = ((), (), s32[]{:S(2)}) async-start(), calls=%async_computation.15 | async-start | bytes 51249152 | tf_op jit(solution)/shard_map/reduce_scatter | solution.py:339
  1288.5 1000.4 %all-reduce.32.cloned.1.call-start = ((), (), s32[]{:S(2)}) async-start(), calls=%async_computation.17 | async-start | bytes 20971520 | tf_op jit(solution)/shard_map/psum | solution.py:341
  2292.1 5.7 copy-start.1
  (102 other events, 282.9 us)
Sparse Core Ops, SparseCore 0:
  9.6 239.8 all-gather.1
  805.4 41.6 reduce-scatter.7
  940.5 42.9 reduce-scatter.5
  1077.1 27.1 reduce-scatter.9
  1173.7 450.9 reduce-scatter.13
  1629.5 449.4 reduce-scatter.11
  2086.2 202.6 all-reduce.31
